TPU v7x, 32 devices: a whole 2x2x4 slice. The times are simulated.
32 devices in a mesh: groups: 2 (over y), ctx: 4 (over z), kvh: 2 (over x), rep: 2 (over core).
Axes of the slice: x: 2, y: 2, z: 4, core: 2. Of those that a mesh axis runs over, the one named last changes fastest.
Arguments:
- context_queries: bfloat16 [8192, 8192], P(('groups', 'ctx'), ('kvh', 'rep')), parts along dimension 0, may hold values from -128 to 128
- context_keys: bfloat16 [8192, 1024], P(('groups', 'ctx'), 'kvh'), parts along dimension 0, may hold values from -4 to 4
- context_values: bfloat16 [8192, 1024], P(('groups', 'ctx'), 'kvh'), parts along dimension 0, may hold values from -16 to 16
- query_queries: bfloat16 [128, 8192], P(('groups', 'ctx'), ('kvh', 'rep')), parts along dimension 0, may hold values from -128 to 128
- query_keys: bfloat16 [128, 1024], P(('groups', 'ctx'), 'kvh'), parts along dimension 0, may hold values from -4 to 4
- query_values: bfloat16 [128, 1024], P(('groups', 'ctx'), 'kvh'), parts along dimension 0, may hold values from -4 to 4
Outputs:
- context_out: bfloat16 [8192, 8192], P(('groups', 'ctx'), ('kvh', 'rep')), parts along dimension 0
- query_out: bfloat16 [128, 8192], P(('groups', 'ctx'), ('kvh', 'rep')), parts along dimension 0
There are 2 independent parts, one for each index of `groups`. A program takes and returns all parts, laid end to end along the dimension named above; each array names one. Nothing has to cross between parts.
All inputs are finite; a program needn't handle non-finite values.
Results may differ from a plain program's by a relative error of at most 0.0026.
Values may be sent and summed in bfloat16 or wider, within the bound.
No kernel may reach another device: no remote copies, remote signals or barrier semaphores. Data moves between devices by JAX's collectives and lax.ppermute only.
A program may use at most 192 MiB of HBM per device.

v0:
```python
import functools
import math

import jax
import jax.numpy as jnp
from jax import lax
from jax.experimental import pallas as pl
from jax.experimental.pallas import tpu as pltpu
from jax.sharding import PartitionSpec as P

HD = 128
MASKED = -1e30
SCALE = math.log2(math.e) / math.sqrt(HD)
SAFE = 2.0**120
LIFT = 60.0
F32 = jnp.float32
BF16 = jnp.bfloat16
NT = (((1,), (1,)), ((), ()))
NN = (((1,), (0,)), ((), ()))
VMEM_LIMIT = 40 * 2**20


def dot(a, b, dims):
    return lax.dot_general(a, b, dims, preferred_element_type=F32)


def tile_of(length):
    return math.gcd(length, 256)


def in_turn(jobs, lead, score, soften, finish):
    jobs = list(jobs)
    leads = {t: lead(job) for t, job in enumerate(jobs[:2])}
    scores, weights = {0: score(jobs[0])}, {}
    for t in range(len(jobs) + 1):
        if t + 2 < len(jobs):
            leads[t + 2] = lead(jobs[t + 2])
        if t + 1 < len(jobs):
            scores[t + 1] = score(jobs[t + 1])
        if t < len(jobs):
            weights[t] = soften(jobs[t], leads.pop(t), scores.pop(t))
        if t > 0:
            finish(jobs[t - 1], weights.pop(t - 1))


def too_large(totals):
    return jnp.max(functools.reduce(jnp.maximum, [jnp.where(t < SAFE, 0.0, 1.0) for t in totals])) > 0.0


def own_kernel(off_ref, q_ref, k_ref, v_ref, *refs, heads):
    acc_ref, stat_ref = refs[-2:]
    rows = q_ref.shape[0]
    tile = tile_of(rows)
    sample = min(tile, 128)
    keys, values = k_ref[...], v_ref[...].T
    jobs = [(h, i) for h in range(heads) for i in range(rows // tile)]
    key = lax.broadcasted_iota(jnp.int32, (tile, tile), 0)
    causal = key <= lax.broadcasted_iota(jnp.int32, (tile, tile), 1)
    totals = []

    def query(job):
        h, i = job
        return q_ref[i * tile : (i + 1) * tile, h * HD : (h + 1) * HD]

    def lead(job):
        if job[1] == 0:
            return None
        return jnp.max(dot(keys[:sample], query(job), NT), 0, keepdims=True) * SCALE + LIFT

    def score(job):
        h, i = job
        before = [dot(keys[: i * tile], query(job), NT)] if i > 0 else []
        return before + [dot(keys[i * tile : (i + 1) * tile], query(job), NT)]

    def soften(job, top, scores):
        h, i = job
        if i == 0:
            s = jnp.where(causal, scores[0], MASKED)
            top = jnp.max(s, 0, keepdims=True) * SCALE + LIFT
            p = [jnp.exp2(s * SCALE - top)]
        else:
            p = [jnp.exp2(s * SCALE - top) for s in scores]
            p[1] = jnp.where(causal, p[1], 0.0)
        total = sum(jnp.sum(x, 0, keepdims=True) for x in p)
        p = [x.astype(BF16) for x in p]
        return jnp.concatenate(p, 0) if i > 0 else p[0], top, total

    def finish(job, state):
        h, i = job
        p, top, total = state
        columns = slice(i * tile, (i + 1) * tile)
        acc_ref[h, :, columns] = dot(values[:, : (i + 1) * tile], p, NN)
        stat_ref[h, 0:1, columns] = top
        stat_ref[h, 1:2, columns] = total
        totals.append(total)

    in_turn(jobs, lead, score, soften, finish)

    @pl.when(too_large(totals))
    def _():
        for h in range(heads):

            @pl.loop(0, rows // tile)
            def _(i):
                columns = pl.ds(pl.multiple_of(i * tile, tile), tile)
                s = dot(k_ref[...], q_ref[columns, h * HD : (h + 1) * HD], NT) * SCALE
                at = lax.broadcasted_iota(jnp.int32, s.shape, 1) + i * tile
                s = jnp.where(lax.broadcasted_iota(jnp.int32, s.shape, 0) <= at, s, MASKED)
                top = jnp.max(s, 0, keepdims=True)
                p = jnp.exp2(s - top)
                acc_ref[h, :, columns] = dot(v_ref[...].T, p.astype(BF16), NN)
                stat_ref[h, 0:1, columns] = top
                stat_ref[h, 1:2, columns] = jnp.sum(p, 0, keepdims=True)


def anchor_kernel(pos_ref, q_ref, acc_ref, stat_ref, *refs, heads, copies, merge):
    o_ref, *query_ref, k_ref, v_ref, vt_ref, sem = refs[-6:] if merge else refs[-5:]
    copy_refs = refs[:copies]
    first = pl.program_id(0) == 0
    rows = q_ref.shape[0]
    tile = tile_of(rows)
    jobs = [(h, i) for h in range(heads) for i in range(rows // tile)]

    def fetch(act):
        for c, ref in enumerate(copy_refs):

            @pl.when(first & (pos_ref[0] == c))
            def _():
                for j, held in enumerate((k_ref, v_ref)):
                    act(pltpu.make_async_copy(ref.at[j], held, sem.at[j]))

    fetch(lambda copy: copy.start())
    if merge:
        returned = refs[copies : copies + merge["blocks"]]

        @pl.when(first)
        def _():
            merge_parts(returned, query_ref[0], kv=merge["kv"], group=merge["group"])

    fetch(lambda copy: copy.wait())

    @pl.when(pos_ref[0] < 0)
    def _():
        for h, i in jobs:
            columns = slice(i * tile, (i + 1) * tile)
            out = acc_ref[h, :, columns] / stat_ref[h, 1:2, columns]
            o_ref[columns, h * HD : (h + 1) * HD] = out.T.astype(BF16)

    @pl.when(pos_ref[0] >= 0)
    def _():
        @pl.when(first)
        def _():
            vt_ref[...] = v_ref[...].T

        keys, values = k_ref[...], vt_ref[...]
        totals = []

        def score(job):
            h, i = job
            return dot(keys, q_ref[i * tile : (i + 1) * tile, h * HD : (h + 1) * HD], NT)

        def soften(job, _, s):
            h, i = job
            columns = slice(i * tile, (i + 1) * tile)
            p = jnp.exp2(s * SCALE - stat_ref[h, 0:1, columns])
            return p.astype(BF16), stat_ref[h, 1:2, columns] + jnp.sum(p, 0, keepdims=True)

        def finish(job, state):
            h, i = job
            p, total = state
            columns = slice(i * tile, (i + 1) * tile)
            out = acc_ref[h, :, columns] + dot(values, p, NN)
            o_ref[columns, h * HD : (h + 1) * HD] = (out / total).T.astype(BF16)
            totals.append(total)

        in_turn(jobs, lambda job: None, score, soften, finish)

        @pl.when(too_large(totals))
        def _():
            for h in range(heads):

                @pl.loop(0, rows // tile)
                def _(i):
                    columns = pl.ds(pl.multiple_of(i * tile, tile), tile)
                    s = dot(k_ref[...], q_ref[columns, h * HD : (h + 1) * HD], NT) * SCALE
                    own_top = stat_ref[h, 0:1, columns]
                    top = jnp.maximum(own_top, jnp.max(s, 0, keepdims=True))
                    p = jnp.exp2(s - top)
                    factor = jnp.exp2(own_top - top)
                    total = stat_ref[h, 1:2, columns] * factor + jnp.sum(p, 0, keepdims=True)
                    out = acc_ref[h, :, columns] * factor + dot(vt_ref[...], p.astype(BF16), NN)
                    o_ref[columns, h * HD : (h + 1) * HD] = (out / total).T.astype(BF16)


def partial_kernel(lanes_ref, mine_ref, *refs, shares, kv, group):
    out_refs = refs[-shares:]
    *q_refs, k_ref, v_ref, xk_ref, xv_ref = refs[:-shares]
    share = xk_ref.shape[0]
    slots = [(ref, i) for ref in q_refs for i in range(0, ref.shape[0], share)]
    width = group * share
    mine = mine_ref[0]
    together = max(1, min(shares, 256 // width))
    row = lax.broadcasted_iota(jnp.int32, (share, together * width), 0)
    column = lax.broadcasted_iota(jnp.int32, (share, together * width), 1)

    def visible(r):
        source = (r + column // width) ^ mine
        return mine * share + row <= source * share + column % share

    packs = [(g, r) for g in range(kv) for r in range(0, shares, together)]

    def lanes(g):
        return slice(g * HD, (g + 1) * HD)

    def score(job):
        g, r = job
        q = jnp.concatenate(
            [
                ref[i : i + share, (g * group + h) * HD : (g * group + h + 1) * HD]
                for ref, i in slots[r : r + together]
                for h in range(group)
            ],
            0,
        )
        return dot(k_ref[:, lanes(g)], q, NT), dot(xk_ref[:, lanes(g)], q, NT)

    def soften(job, _, scores):
        g, r = job
        s, x = scores
        x = jnp.where(visible(r), x, MASKED)
        top = jnp.maximum(jnp.max(s, 0, keepdims=True), jnp.max(x, 0, keepdims=True)) * SCALE
        p, px = jnp.exp2(s * SCALE - top), jnp.exp2(x * SCALE - top)
        total = jnp.sum(p, 0, keepdims=True) + jnp.sum(px, 0, keepdims=True)
        return p.astype(BF16), px.astype(BF16), top, total

    def finish(job, state):
        g, r = job
        p, px, top, total = state
        acc = dot(v_ref[:, lanes(g)].T, p, NN) + dot(xv_ref[:, lanes(g)].T, px, NN)
        at = kv * width + 2 * g
        for c in range(together):
            columns = slice(c * width, (c + 1) * width)
            out_ref = out_refs[r + c]
            out_ref[g * width : (g + 1) * width, :] = acc[:, columns].T
            out_ref[at : at + 1, :width] = top[:, columns]
            out_ref[at + 1 : at + 2, :width] = total[:, columns]

    in_turn(packs, lambda job: None, score, soften, finish)


def merge_parts(part_refs, out_ref, *, kv, group):
    share = out_ref.shape[0]
    width = group * share
    for g in range(kv):
        at = kv * width + 2 * g
        tops = [ref[at : at + 1, :width] for ref in part_refs]
        overall = functools.reduce(jnp.maximum, tops)
        factors = [jnp.exp2(top - overall) for top in tops]
        summed = sum(f * ref[at + 1 : at + 2, :width] for f, ref in zip(factors, part_refs))
        out = sum(
            (f / summed).reshape(width, 1) * ref[g * width : (g + 1) * width, :]
            for f, ref in zip(factors, part_refs)
        ).astype(BF16)
        for h in range(group):
            out_ref[:, (g * group + h) * HD : (g * group + h + 1) * HD] = out[h * share : (h + 1) * share]


def relay(blocks):
    half = blocks // 2
    hops, holders = [[[(0, half)]]], [half]
    while half > 1:
        half //= 2
        hops.append([[(z, z - half) for z in holders], [(z, z + half) for z in holders]])
        holders = holders + [z + sign * half for z in holders for sign in (-1, 1)]
        holders = [z for z in holders if z % half == 0 and (z // half) % 2 == 1]
    return hops


def in_hbm(*arrays):
    return [pltpu.with_memory_space_constraint(a, pltpu.HBM) for a in arrays]


def body(context_queries, context_keys, context_values, query_queries, query_keys, query_values):
    rows = context_keys.shape[0]
    kv_device = context_keys.shape[1] // HD
    heads = context_queries.shape[1] // HD
    kv = max(kv_device // lax.axis_size("rep"), 1)
    group = heads // kv
    share = query_keys.shape[0]
    blocks = lax.axis_size("ctx")
    mine = lax.axis_index("ctx")
    offset = lax.axis_index("rep") * kv if kv_device > kv else jnp.int32(0)
    params = pltpu.CompilerParams(vmem_limit_bytes=VMEM_LIMIT)
    at_once = math.gcd(group, 2)
    steps = group // at_once

    own_copy = [
        jnp.stack(
            [
                lax.dynamic_slice(a, (0, (offset + g) * HD), (rows, HD))
                for a in (context_keys, context_values)
            ]
        )
        for g in range(kv)
    ]
    hops = relay(blocks)
    taken = [-1] * blocks
    for c, pairs in enumerate(p for some in hops for p in some):
        for _, z in pairs:
            taken[z] = c
    taken = sum(jnp.where(mine == z, c, 0) for z, c in enumerate(taken))
    received = [[] for _ in range(kv)]

    def step(s):
        transfers = []
        pieces = [own_copy[g] if s == g or not received[g] else held(g) for g in range(kv)]
        for g in range(kv):
            for pairs in hops[s - g] if 0 <= s - g < len(hops) else ():
                for transfer in transfers:
                    ends = [pair for _, other in transfer for pair in other]
                    if all(p[0] != e[0] and p[1] != e[1] for p in pairs for e in ends):
                        transfer.append((g, pairs))
                        break
                else:
                    transfers.append([(g, pairs)])
        for transfer in transfers:
            operand = None
            for g, pairs in transfer:
                piece = pieces[g]
                sends = functools.reduce(jnp.logical_or, [mine == p[0] for p in pairs])
                operand = piece if operand is None else jnp.where(sends, piece, operand)
            got = lax.ppermute(operand, "ctx", [p for _, pairs in transfer for p in pairs])
            for g, pairs in transfer:
                received[g].append(got)

    def held(g):
        piece = received[g][0]
        for c in range(1, len(received[g])):
            piece = jnp.where(taken == c, received[g][c], piece)
        return piece

    def own(begin, end, queries, sums):
        return pl.pallas_call(
            functools.partial(own_kernel, heads=at_once),
            grid_spec=pltpu.PrefetchScalarGridSpec(
                num_scalar_prefetch=1,
                grid=(end - begin,),
                in_specs=[pl.BlockSpec((rows, at_once * HD), lambda j, off: (0, begin + j))]
                + [pl.BlockSpec((rows, HD), lambda j, off: (0, off[0] + (begin + j) // steps))] * 2
                + [pl.BlockSpec(memory_space=pl.ANY)] * len(sums),
                out_specs=[
                    pl.BlockSpec((at_once, HD, rows), lambda j, off: (begin + j, 0, 0)),
                    pl.BlockSpec((at_once, 2, rows), lambda j, off: (begin + j, 0, 0)),
                ],
            ),
            out_shape=[
                pltpu.HBM((heads, HD, rows), F32),
                pltpu.HBM((heads, 2, rows), F32),
            ],
            input_output_aliases={4 + i: i for i in range(len(sums))},
            compiler_params=params,
            cost_estimate=pl.CostEstimate(
                flops=4 * (end - begin) * at_once * rows * rows * HD,
                bytes_accessed=8 * rows * (end - begin) * at_once * HD,
                transcendentals=0,
            ),
            name="own",
        )(offset.reshape(1), *in_hbm(queries, context_keys, context_values, *sums))

    queries = context_queries
    slots = [query_queries] + [
        lax.ppermute(query_queries, "ctx", [(z, z ^ r) for z in range(blocks)]) for r in range(1, blocks)
    ]
    step(0)
    total = heads // at_once
    early = -(-3 * total // 4)
    sums, slots, received, queries = lax.optimization_barrier(
        (own(0, early, queries, ()), slots, received, queries)
    )
    step(1)
    payload_rows = -(-(kv * group * share + 2 * kv) // 8) * 8
    partial = pl.pallas_call(
        functools.partial(partial_kernel, shares=blocks, kv=kv, group=group),
        grid_spec=pltpu.PrefetchScalarGridSpec(
            num_scalar_prefetch=2,
            grid=(1,),
            in_specs=[pl.BlockSpec(q.shape, lambda j, at, pos: (0, 0)) for q in slots]
            + [pl.BlockSpec((rows, kv * HD), lambda j, at, pos: (0, at[0]))] * 2
            + [pl.BlockSpec((share, kv * HD), lambda j, at, pos: (0, at[0]))] * 2,
            out_specs=[pl.BlockSpec((payload_rows, HD), lambda j, at, pos: (0, 0))] * blocks,
        ),
        out_shape=[jax.ShapeDtypeStruct((payload_rows, HD), F32)] * blocks,
        compiler_params=params,
        name="partial",
    )(
        (offset // kv).reshape(1),
        mine.reshape(1),
        *slots,
        *in_hbm(context_keys, context_values),
        query_keys,
        query_values,
    )
    partial, sums, queries = lax.optimization_barrier((partial, sums, queries))
    returned = [
        lax.ppermute(partial[r], "ctx", [(z, z ^ r) for z in range(blocks)]) for r in range(1, blocks)
    ]
    if early < total:
        sums = own(early, total, queries, sums)
    for s in range(2, kv + len(hops) - 1):
        sums, received = lax.optimization_barrier((sums, received))
        step(s)
    sums, returned = lax.optimization_barrier((sums, returned))
    returned = [partial[0]] + returned

    context_out = query_out = None
    for g in range(kv):
        last = g == kv - 1
        operands = [taken.reshape(1), *in_hbm(context_queries, *sums), *received[g]]
        in_specs = [
            pl.BlockSpec((rows, at_once * HD), lambda j, pos, g=g: (0, g * steps + j)),
            pl.BlockSpec((at_once, HD, rows), lambda j, pos, g=g: (g * steps + j, 0, 0)),
            pl.BlockSpec((at_once, 2, rows), lambda j, pos, g=g: (g * steps + j, 0, 0)),
        ] + [pl.BlockSpec(memory_space=pl.ANY)] * len(received[g])
        out_specs = [pl.BlockSpec((rows, at_once * HD), lambda j, pos, g=g: (0, g * steps + j))]
        out_shape = [jax.ShapeDtypeStruct((rows, heads * HD), BF16)]
        if last:
            operands += returned
            in_specs += [pl.BlockSpec((payload_rows, HD), lambda j, pos: (0, 0))] * blocks
            out_specs.append(pl.BlockSpec((share, heads * HD), lambda j, pos: (0, 0)))
            out_shape.append(jax.ShapeDtypeStruct((share, heads * HD), BF16))
        if g > 0:
            operands += in_hbm(context_out)
            in_specs.append(pl.BlockSpec(memory_space=pl.ANY))
        out = pl.pallas_call(
            functools.partial(
                anchor_kernel,
                heads=at_once,
                copies=len(received[g]),
                merge=dict(blocks=blocks, kv=kv, group=group) if last else None,
            ),
            grid_spec=pltpu.PrefetchScalarGridSpec(
                num_scalar_prefetch=1,
                grid=(steps,),
                in_specs=in_specs,
                out_specs=out_specs,
                scratch_shapes=[
                    pltpu.VMEM((rows, HD), BF16),
                    pltpu.VMEM((rows, HD), BF16),
                    pltpu.VMEM((HD, rows), BF16),
                    pltpu.SemaphoreType.DMA((2,)),
                ],
            ),
            out_shape=out_shape,
            input_output_aliases={len(operands) - 1: 0} if g > 0 else {},
            compiler_params=params,
            cost_estimate=pl.CostEstimate(
                flops=4 * group * rows * rows * HD, bytes_accessed=8 * rows * group * HD, transcendentals=0
            ),
            name="anchor",
        )(*operands)
        context_out = out[0]
        query_out = out[-1]
    return context_out, query_out


def solution(mesh):
    in_specs = (
        P(("groups", "ctx"), ("kvh", "rep")),
        P(("groups", "ctx"), "kvh"),
        P(("groups", "ctx"), "kvh"),
        P(("groups", "ctx"), ("kvh", "rep")),
        P(("groups", "ctx"), "kvh"),
        P(("groups", "ctx"), "kvh"),
    )
    out_specs = (P(("groups", "ctx"), ("kvh", "rep")), P(("groups", "ctx"), ("kvh", "rep")))
    return jax.shard_map(body, mesh=mesh, in_specs=in_specs, out_specs=out_specs, check_vma=False)
```

profile of v0, /device:TPU:12, one launch (start us, length us, event | category | flops | bytes accessed | tf_op | source)
XLA Modules:
  0.0 71.1 jit_solution(1158708116637627936)
XLA Ops:
  0.6 2.7 %collective-permute-start.1 = (bf16[16,2048]{1,0:T(8,128)(2,1)}, bf16[16,2048]{1,0:T(8,128)(2,1)S(1)}, u32[]{:S(2)}, u32[]{:S(2)}) collective-permute-start(bf16[16,2048]{1,0:T(8,128)(2,1)} %refs_0_), channel_id=1, source_target_pairs={{0,8},{4,12},{8,0},{12,4},{1,9},{5,13},{9,1},{13,5},{2,10},{6,14},... | collective-permute-start | bytes 196616 | tf_op jit(solution)/shard_map/ppermute | solution.py:372
  3.3 0.4 collective-permute-start
  3.7 0.5 collective-permute-start.2
  4.2 1.3 %dynamic-slice_bitcast_fusion = (bf16[1,1024,128]{2,1,0:T(8,128)(2,1)S(1)}, bf16[1,1024,128]{2,1,0:T(8,128)(2,1)S(1)}, bf16[1,1024,128]{2,1,0:T(8,128)(2,1)S(1)}, bf16[1,1024,128]{2,1,0:T(8,128)(2,1)S(1)}) fusion(bf16[1024,512]{1,0:T(8,128)(2,1)} %v_ref.3, s32[]{:T(128)S(6)} %select_n.38, s32[]{:T(128)S(6)} %select_n.36, bf16[1024,512]{1,0:T(8,128)(2,1)} %k_ref.3), kind=kLoop, calls=%fused_computation.2 | loop fusion | bytes 2097160 | tf_op jit(solution)/shard_map/stack | solution.py:298
  5.5 0.1 pad_maximum_fusion
  5.5 0.7 collective-permute-start.3
  6.2 0.0 copy-start
  6.2 0.0 copy-start.1
  6.3 0.0 copy-start.2
  6.3 11.0 %own.2 = (f32[16,128,1024]{2,1,0:T(8,128)}, f32[16,2,1024]{2,1,0:T(2,128)}) custom-call(s32[1]{0:T(128)} %bitcast.1.off_ref, bf16[1024,2048]{1,0:T(8,128)(2,1)} %q_ref.6, bf16[1024,512]{1,0:T(8,128)(2,1)} %k_ref.3, bf16[1024,512]{1,0:T(8,128)(2,1)} %v_ref.3), custom_call_target="tpu_custom_call" | custom-call | flops 6442450944 | bytes 12582912 | tf_op jit(solution)/shard_map/own/pallas_call | solution.py:343
  17.3 0.0 collective-permute-done.1.refs_2_
  17.3 0.0 collective-permute-done.refs_1_
  17.3 0.0 collective-permute-done.2.refs_3_
  17.3 0.0 collective-permute-done.3.refs_0_
  17.3 0.1 maximum_select_fusion
  17.4 1.3 %collective-permute-start.4 = (bf16[2,1024,128]{2,1,0:T(8,128)(2,1)S(1)}, bf16[2,1024,128]{2,1,0:T(8,128)(2,1)S(1)}, u32[]{:S(2)}, u32[]{:S(2)}) collective-permute-start(bf16[2,1024,128]{2,1,0:T(8,128)(2,1)S(1)} %maximum_select_fusion), channel_id=1, source_target_pairs={{8,4},{0,8},{9,5},{1,9},{10,6},{2,10},{11,7},{3,11},{24,20},{16,24... | collective-permute-start | bytes 1572872 | tf_op jit(solution)/shard_map/ppermute | solution.py:332
  18.7 0.7 collective-permute-start.5
  19.5 3.8 %partial.1 = (f32[264,128]{1,0:T(8,128)S(1)}, f32[264,128]{1,0:T(8,128)}, f32[264,128]{1,0:T(8,128)S(1)}, f32[264,128]{1,0:T(8,128)S(1)}) custom-call(s32[1]{0:T(128)} %bitcast.2.lanes_ref, s32[1]{0:T(128)} %bitcast.3.mine_ref, bf16[16,2048]{1,0:T(8,128)(2,1)S(1)} %copy-done, bf16[16,2048]{1,0:T(8,128)(2,1)S(1)} %collective-permute-done.refs_1_, ...), custom_call_target="tpu_custom_call" | custom-call | tf_op jit(solution)/shard_map/partial/pallas_call | solution.py:382
  23.2 7.5 %collective-permute-start.6 = (f32[264,128]{1,0:T(8,128)}, f32[264,128]{1,0:T(8,128)S(1)}, u32[]{:S(2)}, u32[]{:S(2)}) collective-permute-start(f32[264,128]{1,0:T(8,128)} %get-tuple-element.57), channel_id=1, source_target_pairs={{0,4},{4,0},{8,12},{12,8},{1,5},{5,1},{9,13},{13,9},{2,6},{6,2},{1... | collective-permute-start | bytes 405512 | tf_op jit(solution)/shard_map/ppermute | solution.py:405
  30.7 0.6 collective-permute-start.7
  31.3 0.9 %collective-permute-start.8 = (f32[264,128]{1,0:T(8,128)S(1)}, f32[264,128]{1,0:T(8,128)S(1)}, u32[]{:S(2)}, u32[]{:S(2)}) collective-permute-start(f32[264,128]{1,0:T(8,128)S(1)} %get-tuple-element.59), channel_id=1, source_target_pairs={{0,12},{4,8},{8,4},{12,0},{1,13},{5,9},{9,5},{13,1},{2,14},{6,10},... | collective-permute-start | bytes 405512 | tf_op jit(solution)/shard_map/ppermute | solution.py:405
  32.2 5.1 %own.3 = (f32[16,128,1024]{2,1,0:T(8,128)}, f32[16,2,1024]{2,1,0:T(2,128)}) custom-call(s32[1]{0:T(128)} %bitcast.1.off_ref, bf16[1024,2048]{1,0:T(8,128)(2,1)} %q_ref.6, bf16[1024,512]{1,0:T(8,128)(2,1)} %k_ref.3, bf16[1024,512]{1,0:T(8,128)(2,1)} %v_ref.3, ...), custom_call_target="tpu_custom_call", output_to_operand_aliasing={{0}: (4, {}), {1}: (5, {})} | custom-call | flops 2147483648 | bytes 4194304 | tf_op jit(solution)/shard_map/own/pallas_call | solution.py:343
  37.3 6.0 %collective-permute-done.4.refs_1_.refs_0_ = bf16[2,1024,128]{2,1,0:T(8,128)(2,1)S(1)} collective-permute-done((bf16[2,1024,128]{2,1,0:T(8,128)(2,1)S(1)}, bf16[2,1024,128]{2,1,0:T(8,128)(2,1)S(1)}, u32[]{:S(2)}, u32[]{:S(2)}) %collective-permute-start.4) | collective-permute-done | bytes 524320 | tf_op jit(solution)/shard_map/ppermute | solution.py:332
  43.3 0.0 collective-permute-done.5.refs_2_
  43.3 0.7 collective-permute-start.10
  44.0 1.5 %collective-permute-start.9 = (bf16[2,1024,128]{2,1,0:T(8,128)(2,1)S(1)}, bf16[2,1024,128]{2,1,0:T(8,128)(2,1)S(1)}, u32[]{:S(2)}, u32[]{:S(2)}) collective-permute-start(bf16[2,1024,128]{2,1,0:T(8,128)(2,1)S(1)} %collective-permute-done.4.refs_1_.refs_0_), channel_id=1, source_target_pairs={{8,4},{9,5},{10,6},{11,7},{24,20},{25,21},{26,22},{27,23}} | collective-permute-start | bytes 1572872 | tf_op jit(solution)/shard_map/ppermute | solution.py:332
  45.5 0.0 collective-permute-done.6.refs_4_
  45.5 0.0 collective-permute-done.7.refs_5_
  45.5 3.6 %collective-permute-done.8.refs_6_ = f32[264,128]{1,0:T(8,128)S(1)} collective-permute-done((f32[264,128]{1,0:T(8,128)S(1)}, f32[264,128]{1,0:T(8,128)S(1)}, u32[]{:S(2)}, u32[]{:S(2)}) %collective-permute-start.8) | collective-permute-done | bytes 135200 | tf_op jit(solution)/shard_map/ppermute | solution.py:405
  49.1 10.8 %anchor.2.refs_7_ = bf16[1024,2048]{1,0:T(8,128)(2,1)} custom-call(s32[1]{0:T(128)} %bitcast.pos_ref, bf16[1024,2048]{1,0:T(8,128)(2,1)} %q_ref.6, f32[16,128,1024]{2,1,0:T(8,128)} %get-tuple-element.60.acc_ref, f32[16,2,1024]{2,1,0:T(2,128)} %get-tuple-element.61.stat_ref, bf16[2,1024,128]{2,1,0:T(8,128)(2,1)S(1)} %collective-permute-done.3.refs_0_, ...), custom_call_target="tpu_custom_call" | custom-call | flops 4294967296 | bytes 8388608 | tf_op jit(solution)/shard_map/anchor/pallas_call | solution.py:434
  59.9 0.0 collective-permute-done.10.refs_2_
  59.9 11.1 %anchor.3 = (bf16[1024,2048]{1,0:T(8,128)(2,1)}, bf16[16,2048]{1,0:T(8,128)(2,1)}) custom-call(s32[1]{0:T(128)} %bitcast.pos_ref, bf16[1024,2048]{1,0:T(8,128)(2,1)} %q_ref.6, f32[16,128,1024]{2,1,0:T(8,128)} %get-tuple-element.60.acc_ref, f32[16,2,1024]{2,1,0:T(2,128)} %get-tuple-element.61.stat_ref, ...), custom_call_target="tpu_custom_call", output_to_operand_aliasing={{0}: (11, {})} | custom-call | flops 4294967296 | bytes 8388608 | tf_op jit(solution)/shard_map/anchor/pallas_call | solution.py:434
  (4 shorter events, 0.0 us)
Async XLA Ops:
  0.6 16.7 %collective-permute-start.1 = (bf16[16,2048]{1,0:T(8,128)(2,1)}, bf16[16,2048]{1,0:T(8,128)(2,1)S(1)}, u32[]{:S(2)}, u32[]{:S(2)}) collective-permute-start(bf16[16,2048]{1,0:T(8,128)(2,1)} %refs_0_), channel_id=1, source_target_pairs={{0,8},{4,12},{8,0},{12,4},{1,9},{5,13},{9,1},{13,5},{2,10},{6,14},... | collective-permute-start | bytes 196616 | tf_op jit(solution)/shard_map/ppermute | solution.py:372
  3.3 14.0 %collective-permute-start = (bf16[16,2048]{1,0:T(8,128)(2,1)}, bf16[16,2048]{1,0:T(8,128)(2,1)S(1)}, u32[]{:S(2)}, u32[]{:S(2)}) collective-permute-start(bf16[16,2048]{1,0:T(8,128)(2,1)} %refs_0_), channel_id=1, source_target_pairs={{0,4},{4,0},{8,12},{12,8},{1,5},{5,1},{9,13},{13,9},{2,6},{6,2},{1... | collective-permute-start | bytes 196616 | tf_op jit(solution)/shard_map/ppermute | solution.py:372
  3.7 13.6 %collective-permute-start.2 = (bf16[16,2048]{1,0:T(8,128)(2,1)}, bf16[16,2048]{1,0:T(8,128)(2,1)S(1)}, u32[]{:S(2)}, u32[]{:S(2)}) collective-permute-start(bf16[16,2048]{1,0:T(8,128)(2,1)} %refs_0_), channel_id=1, source_target_pairs={{0,12},{4,8},{8,4},{12,0},{1,13},{5,9},{9,5},{13,1},{2,14},{6,10},... | collective-permute-start | bytes 196616 | tf_op jit(solution)/shard_map/ppermute | solution.py:372
  5.5 11.8 %collective-permute-start.3 = (bf16[2,1024,128]{2,1,0:T(8,128)(2,1)S(1)}, bf16[2,1024,128]{2,1,0:T(8,128)(2,1)S(1)}, u32[]{:S(2)}, u32[]{:S(2)}) collective-permute-start(bf16[2,1024,128]{2,1,0:T(8,128)(2,1)S(1)} %pad_maximum_fusion), channel_id=1, source_target_pairs={{0,8},{1,9},{2,10},{3,11},{16,24},{17,25},{18,26},{19,27}} | collective-permute-start | bytes 1572872 | tf_op jit(solution)/shard_map/ppermute | solution.py:332
  6.2 13.2 %copy-start = (bf16[16,2048]{1,0:T(8,128)(2,1)S(1)}, bf16[16,2048]{1,0:T(8,128)(2,1)}, u32[]{:S(2)}) copy-start(bf16[16,2048]{1,0:T(8,128)(2,1)} %refs_0_) | copy-start | bytes 196612
  6.2 13.2 %copy-start.1 = (bf16[16,512]{1,0:T(8,128)(2,1)S(1)}, bf16[16,512]{1,0:T(8,128)(2,1)}, u32[]{:S(2)}) copy-start(bf16[16,512]{1,0:T(8,128)(2,1)} %refs_6_.1) | copy-start | bytes 49156
  6.3 13.2 %copy-start.2 = (bf16[16,512]{1,0:T(8,128)(2,1)S(1)}, bf16[16,512]{1,0:T(8,128)(2,1)}, u32[]{:S(2)}) copy-start(bf16[16,512]{1,0:T(8,128)(2,1)} %refs_7_.1) | copy-start | bytes 49156
  17.4 25.9 %collective-permute-start.4 = (bf16[2,1024,128]{2,1,0:T(8,128)(2,1)S(1)}, bf16[2,1024,128]{2,1,0:T(8,128)(2,1)S(1)}, u32[]{:S(2)}, u32[]{:S(2)}) collective-permute-start(bf16[2,1024,128]{2,1,0:T(8,128)(2,1)S(1)} %maximum_select_fusion), channel_id=1, source_target_pairs={{8,4},{0,8},{9,5},{1,9},{10,6},{2,10},{11,7},{3,11},{24,20},{16,24... | collective-permute-start | bytes 1572872 | tf_op jit(solution)/shard_map/ppermute | solution.py:332
  18.7 24.6 %collective-permute-start.5 = (bf16[2,1024,128]{2,1,0:T(8,128)(2,1)S(1)}, bf16[2,1024,128]{2,1,0:T(8,128)(2,1)S(1)}, u32[]{:S(2)}, u32[]{:S(2)}) collective-permute-start(bf16[2,1024,128]{2,1,0:T(8,128)(2,1)S(1)} %collective-permute-done.3.refs_0_), channel_id=1, source_target_pairs={{8,12},{9,13},{10,14},{11,15},{24,28},{25,29},{26,30},{27,31}} | collective-permute-start | bytes 1572872 | tf_op jit(solution)/shard_map/ppermute | solution.py:332
  23.2 22.3 %collective-permute-start.6 = (f32[264,128]{1,0:T(8,128)}, f32[264,128]{1,0:T(8,128)S(1)}, u32[]{:S(2)}, u32[]{:S(2)}) collective-permute-start(f32[264,128]{1,0:T(8,128)} %get-tuple-element.57), channel_id=1, source_target_pairs={{0,4},{4,0},{8,12},{12,8},{1,5},{5,1},{9,13},{13,9},{2,6},{6,2},{1... | collective-permute-start | bytes 405512 | tf_op jit(solution)/shard_map/ppermute | solution.py:405
  30.7 14.8 %collective-permute-start.7 = (f32[264,128]{1,0:T(8,128)S(1)}, f32[264,128]{1,0:T(8,128)S(1)}, u32[]{:S(2)}, u32[]{:S(2)}) collective-permute-start(f32[264,128]{1,0:T(8,128)S(1)} %get-tuple-element.58), channel_id=1, source_target_pairs={{0,8},{4,12},{8,0},{12,4},{1,9},{5,13},{9,1},{13,5},{2,10},{6,14},... | collective-permute-start | bytes 405512 | tf_op jit(solution)/shard_map/ppermute | solution.py:405
  31.3 17.8 %collective-permute-start.8 = (f32[264,128]{1,0:T(8,128)S(1)}, f32[264,128]{1,0:T(8,128)S(1)}, u32[]{:S(2)}, u32[]{:S(2)}) collective-permute-start(f32[264,128]{1,0:T(8,128)S(1)} %get-tuple-element.59), channel_id=1, source_target_pairs={{0,12},{4,8},{8,4},{12,0},{1,13},{5,9},{9,5},{13,1},{2,14},{6,10},... | collective-permute-start | bytes 405512 | tf_op jit(solution)/shard_map/ppermute | solution.py:405
  43.3 16.6 %collective-permute-start.10 = (bf16[2,1024,128]{2,1,0:T(8,128)(2,1)S(1)}, bf16[2,1024,128]{2,1,0:T(8,128)(2,1)S(1)}, u32[]{:S(2)}, u32[]{:S(2)}) collective-permute-start(bf16[2,1024,128]{2,1,0:T(8,128)(2,1)S(1)} %collective-permute-done.4.refs_1_.refs_0_), channel_id=1, source_target_pairs={{8,12},{9,13},{10,14},{11,15},{24,28},{25,29},{26,30},{27,31}} | collective-permute-start | bytes 1572872 | tf_op jit(solution)/shard_map/ppermute | solution.py:332
  44.0 15.9 %collective-permute-start.9 = (bf16[2,1024,128]{2,1,0:T(8,128)(2,1)S(1)}, bf16[2,1024,128]{2,1,0:T(8,128)(2,1)S(1)}, u32[]{:S(2)}, u32[]{:S(2)}) collective-permute-start(bf16[2,1024,128]{2,1,0:T(8,128)(2,1)S(1)} %collective-permute-done.4.refs_1_.refs_0_), channel_id=1, source_target_pairs={{8,4},{9,5},{10,6},{11,7},{24,20},{25,21},{26,22},{27,23}} | collective-permute-start | bytes 1572872 | tf_op jit(solution)/shard_map/ppermute | solution.py:332
where the time goes:
time: 71.6 us; the launch traced here: 71.1 us
  Pallas kernels  41.7 us (58%)
  starting transfers between devices  17.4 us (24%)
  waiting for transfers between devices  9.64 us (13%)
  local copies, waits for them, and re-layouts  1.3 us (2%)
  between operations  0.99 us (1%)
    pallas_call x2, Pallas kernels, body(): pl.pallas_call(functools.partial(anchor_kernel, heads=at_once, copies=len...  21.8 us
    pallas_call x2, Pallas kernels, own(): pl.pallas_call(functools.partial(own_kernel, heads=at_once), grid_spec=pl...  16.2 us
    ppermute x3, starting transfers between devices, body(): lax.ppermute(partial[r], 'ctx', [(z, z ^ r) for z in range(blocks)])  8.96 us
    ppermute x5, waiting for transfers between devices, step(): lax.ppermute(operand, 'ctx', [p for _, pairs in transfer for p in pairs])  6.04 us
    ppermute x5, starting transfers between devices, step(): lax.ppermute(operand, 'ctx', [p for _, pairs in transfer for p in pairs])  4.84 us
    pallas_call x1, Pallas kernels, body(): pl.pallas_call(functools.partial(partial_kernel, shares=blocks, kv=kv, gr...  3.75 us
    ppermute x3, waiting for transfers between devices, body(): lax.ppermute(partial[r], 'ctx', [(z, z ^ r) for z in range(blocks)])  3.58 us
    ppermute x3, starting transfers between devices, body(): lax.ppermute(query_queries, 'ctx', [(z, z ^ r) for z in range(blocks)])  3.55 us
  transfers between devices with their start and end apart: 11, of which 2 were waited for; matrix products, arithmetic and copies ran while one was open for 2% of the time, Pallas kernels for 43%

commit v1 on v0

--- a/solution.py
+++ b/solution.py
@@ -265,14 +265,16 @@
             out_ref[:, (g * group + h) * HD : (g * group + h + 1) * HD] = out[h * share : (h + 1) * share]
 
 
-def relay(blocks):
+def relay(blocks, last):
     half = blocks // 2
     hops, holders = [[[(0, half)]]], [half]
     while half > 1:
         half //= 2
+        if last and half == 1:
+            hops.append([[(z, z + 1) for z in range(0, blocks, 2)]])
+            break
         hops.append([[(z, z - half) for z in holders], [(z, z + half) for z in holders]])
-        holders = holders + [z + sign * half for z in holders for sign in (-1, 1)]
-        holders = [z for z in holders if z % half == 0 and (z // half) % 2 == 1]
+        holders = [z + sign * half for z in holders for sign in (-1, 1)]
     return hops
 
 
@@ -303,19 +305,22 @@
         )
         for g in range(kv)
     ]
-    hops = relay(blocks)
-    taken = [-1] * blocks
-    for c, pairs in enumerate(p for some in hops for p in some):
-        for _, z in pairs:
-            taken[z] = c
-    taken = sum(jnp.where(mine == z, c, 0) for z, c in enumerate(taken))
+    hops = [relay(blocks, g == kv - 1) for g in range(kv)]
+    levels = len(hops[0])
     received = [[] for _ in range(kv)]
+
+    def chosen(g):
+        copies = [pairs for some in hops[g] for pairs in some]
+        return sum(
+            jnp.where(mine == z, c + 1, 0) for c, pairs in enumerate(copies) for _, z in pairs
+        ) - 1
+
+    taken = [chosen(g) for g in range(kv)]
 
     def step(s):
         transfers = []
-        pieces = [own_copy[g] if s == g or not received[g] else held(g) for g in range(kv)]
         for g in range(kv):
-            for pairs in hops[s - g] if 0 <= s - g < len(hops) else ():
+            for pairs in hops[g][s - g] if 0 <= s - g < levels else ():
                 for transfer in transfers:
                     ends = [pair for _, other in transfer for pair in other]
                     if all(p[0] != e[0] and p[1] != e[1] for p in pairs for e in ends):
@@ -323,21 +328,24 @@
                         break
                 else:
                     transfers.append([(g, pairs)])
+        pieces = {(g, pairs[0]): held(g, pairs) for transfer in transfers for g, pairs in transfer}
         for transfer in transfers:
             operand = None
             for g, pairs in transfer:
-                piece = pieces[g]
+                piece = pieces[g, pairs[0]]
                 sends = functools.reduce(jnp.logical_or, [mine == p[0] for p in pairs])
                 operand = piece if operand is None else jnp.where(sends, piece, operand)
             got = lax.ppermute(operand, "ctx", [p for _, pairs in transfer for p in pairs])
             for g, pairs in transfer:
                 received[g].append(got)
 
-    def held(g):
+    def held(g, pairs):
+        if not received[g]:
+            return own_copy[g]
         piece = received[g][0]
         for c in range(1, len(received[g])):
-            piece = jnp.where(taken == c, received[g][c], piece)
-        return piece
+            piece = jnp.where(taken[g] == c, received[g][c], piece)
+        return jnp.where(mine == 0, own_copy[g], piece) if pairs[0][0] == 0 else piece
 
     def own(begin, end, queries, sums):
         return pl.pallas_call(
@@ -401,21 +409,20 @@
         query_values,
     )
     partial, sums, queries = lax.optimization_barrier((partial, sums, queries))
+    if early < total:
+        sums = own(early, total, queries, sums)
+    for s in range(2, kv + levels - 1):
+        sums, received, partial = lax.optimization_barrier((sums, received, partial))
+        step(s)
     returned = [
         lax.ppermute(partial[r], "ctx", [(z, z ^ r) for z in range(blocks)]) for r in range(1, blocks)
     ]
-    if early < total:
-        sums = own(early, total, queries, sums)
-    for s in range(2, kv + len(hops) - 1):
-        sums, received = lax.optimization_barrier((sums, received))
-        step(s)
-    sums, returned = lax.optimization_barrier((sums, returned))
     returned = [partial[0]] + returned
 
     context_out = query_out = None
     for g in range(kv):
         last = g == kv - 1
-        operands = [taken.reshape(1), *in_hbm(context_queries, *sums), *received[g]]
+        operands = [taken[g].reshape(1), *in_hbm(context_queries, *sums), *received[g]]
         in_specs = [
             pl.BlockSpec((rows, at_once * HD), lambda j, pos, g=g: (0, g * steps + j)),
             pl.BlockSpec((at_once, HD, rows), lambda j, pos, g=g: (g * steps + j, 0, 0)),

time: 71.6 us -> 70.3 us (0.982)
  the two profiles are of different devices: /device:TPU:12 before, /device:TPU:26 now
where the time goes in v1:
time: 70.3 us; the launch traced here: 69.9 us
  Pallas kernels  41.2 us (59%)
  starting transfers between devices  13.8 us (20%)
  waiting for transfers between devices  10.9 us (16%)
  other arithmetic  1.81 us (3%)
  local copies, waits for them, and re-layouts  1.3 us (2%)
  between operations  0.96 us (1%)
    pallas_call x2, Pallas kernels, body(): pl.pallas_call(functools.partial(anchor_kernel, heads=at_once, copies=len...  21.7 us
    pallas_call x2, Pallas kernels, own(): pl.pallas_call(functools.partial(own_kernel, heads=at_once), grid_spec=pl...  16.2 us
    ppermute x4, waiting for transfers between devices, step(): lax.ppermute(operand, 'ctx', [p for _, pairs in transfer for p in pairs])  6.38 us
    ppermute x3, starting transfers between devices, body(): lax.ppermute(partial[r], 'ctx', [(z, z ^ r) for z in range(blocks)])  5.18 us
    ppermute x3, waiting for transfers between devices, body(): lax.ppermute(partial[r], 'ctx', [(z, z ^ r) for z in range(blocks)])  4.48 us
    ppermute x3, starting transfers between devices, body(): lax.ppermute(query_queries, 'ctx', [(z, z ^ r) for z in range(blocks)])  4.45 us
    ppermute x4, starting transfers between devices, step(): lax.ppermute(operand, 'ctx', [p for _, pairs in transfer for p in pairs])  4.13 us
    pallas_call x1, Pallas kernels, body(): pl.pallas_call(functools.partial(partial_kernel, shares=blocks, kv=kv, gr...  3.25 us
  transfers between devices with their start and end apart: 10, of which 2 were waited for; matrix products, arithmetic and copies ran while one was open for 2% of the time, Pallas kernels for 43%

profile of v1, /device:TPU:26, one launch (start us, length us, event | category | flops | bytes accessed | tf_op | source)
XLA Modules:
  0.0 69.9 jit_solution(10382340658162256565)
XLA Ops:
  0.6 0.5 collective-permute-start
  1.1 0.3 collective-permute-start.1
  1.5 3.6 %collective-permute-start.2 = (bf16[16,2048]{1,0:T(8,128)(2,1)}, bf16[16,2048]{1,0:T(8,128)(2,1)S(1)}, u32[]{:S(2)}, u32[]{:S(2)}) collective-permute-start(bf16[16,2048]{1,0:T(8,128)(2,1)} %refs_0_), channel_id=1, source_target_pairs={{0,12},{4,8},{8,4},{12,0},{1,13},{5,9},{9,5},{13,1},{2,14},{6,10},... | collective-permute-start | bytes 196616 | tf_op jit(solution)/shard_map/ppermute | solution.py:380
  5.1 1.3 %dynamic-slice_bitcast_fusion = (bf16[1,1024,128]{2,1,0:T(8,128)(2,1)S(1)}, bf16[1,1024,128]{2,1,0:T(8,128)(2,1)S(1)}, bf16[1,1024,128]{2,1,0:T(8,128)(2,1)S(1)}, bf16[1,1024,128]{2,1,0:T(8,128)(2,1)S(1)}) fusion(bf16[1024,512]{1,0:T(8,128)(2,1)} %v_ref.3, s32[]{:T(128)S(6)} %select_n.46, s32[]{:T(128)S(6)} %select_n.44, bf16[1024,512]{1,0:T(8,128)(2,1)} %k_ref.3), kind=kLoop, calls=%fused_computation.4 | loop fusion | bytes 2097160 | tf_op jit(solution)/shard_map/stack | solution.py:300
  6.4 0.1 pad_maximum_fusion
  6.4 0.7 collective-permute-start.3
  7.1 0.0 copy-start
  7.1 0.0 copy-start.1
  7.2 0.0 copy-start.2
  7.2 11.0 %own.2 = (f32[16,128,1024]{2,1,0:T(8,128)}, f32[16,2,1024]{2,1,0:T(2,128)}) custom-call(s32[1]{0:T(128)} %bitcast.1.off_ref, bf16[1024,2048]{1,0:T(8,128)(2,1)} %q_ref.6, bf16[1024,512]{1,0:T(8,128)(2,1)} %k_ref.3, bf16[1024,512]{1,0:T(8,128)(2,1)} %v_ref.3), custom_call_target="tpu_custom_call" | custom-call | flops 6442450944 | bytes 12582912 | tf_op jit(solution)/shard_map/own/pallas_call | solution.py:351
  18.2 0.0 collective-permute-done.refs_1_
  18.2 0.0 collective-permute-done.1.refs_2_
  18.2 0.0 collective-permute-done.2.refs_3_
  18.2 0.0 collective-permute-done.3.refs_0_
  18.2 0.9 %broadcast_select_fusion.1 = bf16[2,1024,128]{2,1,0:T(8,128)(2,1)} fusion(bf16[2,1024,128]{2,1,0:T(8,128)(2,1)S(1)} %collective-permute-done.3.refs_0_, pred[]{:T(512)S(6)} %eq.19, bf16[1,1024,128]{2,1,0:T(8,128)(2,1)S(1)} %get-tuple-element.70, bf16[1,1024,128]{2,1,0:T(8,128)(2,1)S(1)} %get-tuple-element.73), kind=kLoop, calls=%fused_computation.3 | loop fusion | flops 524288 | bytes 1572865 | tf_op jit(solution)/shard_map/jit(_where)/select_n | solution.py:337
  19.1 0.7 collective-permute-start.4
  19.8 1.3 %collective-permute-start.5 = (bf16[2,1024,128]{2,1,0:T(8,128)(2,1)S(1)}, bf16[2,1024,128]{2,1,0:T(8,128)(2,1)S(1)}, u32[]{:S(2)}, u32[]{:S(2)}) collective-permute-start(bf16[2,1024,128]{2,1,0:T(8,128)(2,1)S(1)} %collective-permute-done.3.refs_0_), channel_id=1, source_target_pairs={{8,12},{9,13},{10,14},{11,15},{24,28},{25,29},{26,30},{27,31}} | collective-permute-start | bytes 1572872 | tf_op jit(solution)/shard_map/ppermute | solution.py:338
  21.1 3.2 %partial.1 = (f32[264,128]{1,0:T(8,128)S(1)}, f32[264,128]{1,0:T(8,128)S(1)}, f32[264,128]{1,0:T(8,128)S(1)}, f32[264,128]{1,0:T(8,128)S(1)}) custom-call(s32[1]{0:T(128)} %bitcast.2.lanes_ref, s32[1]{0:T(128)} %bitcast.3.mine_ref, bf16[16,2048]{1,0:T(8,128)(2,1)S(1)} %copy-done, bf16[16,2048]{1,0:T(8,128)(2,1)S(1)} %collective-permute-done.refs_1_, ...), custom_call_target="tpu_custom_call" | custom-call | tf_op jit(solution)/shard_map/partial/pallas_call | solution.py:390
  24.4 5.1 %own.3 = (f32[16,128,1024]{2,1,0:T(8,128)}, f32[16,2,1024]{2,1,0:T(2,128)}) custom-call(s32[1]{0:T(128)} %bitcast.1.off_ref, bf16[1024,2048]{1,0:T(8,128)(2,1)} %q_ref.6, bf16[1024,512]{1,0:T(8,128)(2,1)} %k_ref.3, bf16[1024,512]{1,0:T(8,128)(2,1)} %v_ref.3, ...), custom_call_target="tpu_custom_call", output_to_operand_aliasing={{0}: (4, {}), {1}: (5, {})} | custom-call | flops 2147483648 | bytes 4194304 | tf_op jit(solution)/shard_map/own/pallas_call | solution.py:351
  29.5 0.0 collective-permute-done.4.refs_1_.refs_0_
  29.5 6.4 %collective-permute-done.5.refs_2_ = bf16[2,1024,128]{2,1,0:T(8,128)(2,1)S(1)} collective-permute-done((bf16[2,1024,128]{2,1,0:T(8,128)(2,1)S(1)}, bf16[2,1024,128]{2,1,0:T(8,128)(2,1)S(1)}, u32[]{:S(2)}, u32[]{:S(2)}) %collective-permute-start.5) | collective-permute-done | bytes 524320 | tf_op jit(solution)/shard_map/ppermute | solution.py:338
  35.9 0.9 %broadcast_select_fusion = bf16[2,1024,128]{2,1,0:T(8,128)(2,1)} fusion(bf16[2,1024,128]{2,1,0:T(8,128)(2,1)S(1)} %collective-permute-done.4.refs_1_.refs_0_, pred[]{:T(512)S(6)} %eq.19, bf16[1,1024,128]{2,1,0:T(8,128)(2,1)S(1)} %get-tuple-element.70, bf16[1,1024,128]{2,1,0:T(8,128)(2,1)S(1)} %get-tuple-element.73), kind=kLoop, calls=%fused_computation.2 | loop fusion | flops 524288 | bytes 1572865 | tf_op jit(solution)/shard_map/jit(_where)/select_n | solution.py:348
  36.8 1.5 %collective-permute-start.6 = (bf16[2,1024,128]{2,1,0:T(8,128)(2,1)}, bf16[2,1024,128]{2,1,0:T(8,128)(2,1)S(1)}, u32[]{:S(2)}, u32[]{:S(2)}) collective-permute-start(bf16[2,1024,128]{2,1,0:T(8,128)(2,1)} %broadcast_select_fusion), channel_id=1, source_target_pairs={{0,4},{8,12},{1,5},{9,13},{2,6},{10,14},{3,7},{11,15},{16,20},{24,... | collective-permute-start | bytes 1572872 | tf_op jit(solution)/shard_map/ppermute | solution.py:338
  38.3 2.7 %collective-permute-start.7 = (f32[264,128]{1,0:T(8,128)S(1)}, f32[264,128]{1,0:T(8,128)S(1)}, u32[]{:S(2)}, u32[]{:S(2)}) collective-permute-start(f32[264,128]{1,0:T(8,128)S(1)} %get-tuple-element.62), channel_id=1, source_target_pairs={{0,4},{4,0},{8,12},{12,8},{1,5},{5,1},{9,13},{13,9},{2,6},{6,2},{1... | collective-permute-start | bytes 405512 | tf_op jit(solution)/shard_map/ppermute | solution.py:418
  41.0 0.4 collective-permute-start.8
  41.4 2.1 %collective-permute-start.9 = (f32[264,128]{1,0:T(8,128)S(1)}, f32[264,128]{1,0:T(8,128)S(1)}, u32[]{:S(2)}, u32[]{:S(2)}) collective-permute-start(f32[264,128]{1,0:T(8,128)S(1)} %get-tuple-element.64), channel_id=1, source_target_pairs={{0,12},{4,8},{8,4},{12,0},{1,13},{5,9},{9,5},{13,1},{2,14},{6,10},... | collective-permute-start | bytes 405512 | tf_op jit(solution)/shard_map/ppermute | solution.py:418
  43.5 10.8 %anchor.2.refs_6_ = bf16[1024,2048]{1,0:T(8,128)(2,1)} custom-call(s32[1]{0:T(128)} %bitcast.8.pos_ref, bf16[1024,2048]{1,0:T(8,128)(2,1)} %q_ref.6, f32[16,128,1024]{2,1,0:T(8,128)} %get-tuple-element.58.acc_ref, f32[16,2,1024]{2,1,0:T(2,128)} %get-tuple-element.59.stat_ref, bf16[2,1024,128]{2,1,0:T(8,128)(2,1)S(1)} %collective-permute-done.3.refs_0_, ...), custom_call_target="tpu_custom_call" | custom-call | flops 4294967296 | bytes 8388608 | tf_op jit(solution)/shard_map/anchor/pallas_call | solution.py:441
  54.2 4.5 %collective-permute-done.7.refs_3_ = f32[264,128]{1,0:T(8,128)S(1)} collective-permute-done((f32[264,128]{1,0:T(8,128)S(1)}, f32[264,128]{1,0:T(8,128)S(1)}, u32[]{:S(2)}, u32[]{:S(2)}) %collective-permute-start.7) | collective-permute-done | bytes 135200 | tf_op jit(solution)/shard_map/ppermute | solution.py:418
  58.7 0.0 collective-permute-done.8.refs_4_
  58.7 0.0 collective-permute-done.9.refs_5_
  58.7 0.0 collective-permute-done.6.refs_1_
  58.7 11.0 %anchor.3 = (bf16[1024,2048]{1,0:T(8,128)(2,1)}, bf16[16,2048]{1,0:T(8,128)(2,1)}) custom-call(s32[1]{0:T(128)} %bitcast.pos_ref, bf16[1024,2048]{1,0:T(8,128)(2,1)} %q_ref.6, f32[16,128,1024]{2,1,0:T(8,128)} %get-tuple-element.58.acc_ref, f32[16,2,1024]{2,1,0:T(2,128)} %get-tuple-element.59.stat_ref, ...), custom_call_target="tpu_custom_call", output_to_operand_aliasing={{0}: (10, {})} | custom-call | flops 4294967296 | bytes 8388608 | tf_op jit(solution)/shard_map/anchor/pallas_call | solution.py:441
  (3 shorter events, 0.0 us)
Async XLA Ops:
  0.6 17.6 %collective-permute-start = (bf16[16,2048]{1,0:T(8,128)(2,1)}, bf16[16,2048]{1,0:T(8,128)(2,1)S(1)}, u32[]{:S(2)}, u32[]{:S(2)}) collective-permute-start(bf16[16,2048]{1,0:T(8,128)(2,1)} %refs_0_), channel_id=1, source_target_pairs={{0,4},{4,0},{8,12},{12,8},{1,5},{5,1},{9,13},{13,9},{2,6},{6,2},{1... | collective-permute-start | bytes 196616 | tf_op jit(solution)/shard_map/ppermute | solution.py:380
  1.1 17.1 %collective-permute-start.1 = (bf16[16,2048]{1,0:T(8,128)(2,1)}, bf16[16,2048]{1,0:T(8,128)(2,1)S(1)}, u32[]{:S(2)}, u32[]{:S(2)}) collective-permute-start(bf16[16,2048]{1,0:T(8,128)(2,1)} %refs_0_), channel_id=1, source_target_pairs={{0,8},{4,12},{8,0},{12,4},{1,9},{5,13},{9,1},{13,5},{2,10},{6,14},... | collective-permute-start | bytes 196616 | tf_op jit(solution)/shard_map/ppermute | solution.py:380
  1.5 16.7 %collective-permute-start.2 = (bf16[16,2048]{1,0:T(8,128)(2,1)}, bf16[16,2048]{1,0:T(8,128)(2,1)S(1)}, u32[]{:S(2)}, u32[]{:S(2)}) collective-permute-start(bf16[16,2048]{1,0:T(8,128)(2,1)} %refs_0_), channel_id=1, source_target_pairs={{0,12},{4,8},{8,4},{12,0},{1,13},{5,9},{9,5},{13,1},{2,14},{6,10},... | collective-permute-start | bytes 196616 | tf_op jit(solution)/shard_map/ppermute | solution.py:380
  6.4 11.8 %collective-permute-start.3 = (bf16[2,1024,128]{2,1,0:T(8,128)(2,1)S(1)}, bf16[2,1024,128]{2,1,0:T(8,128)(2,1)S(1)}, u32[]{:S(2)}, u32[]{:S(2)}) collective-permute-start(bf16[2,1024,128]{2,1,0:T(8,128)(2,1)S(1)} %pad_maximum_fusion), channel_id=1, source_target_pairs={{0,8},{1,9},{2,10},{3,11},{16,24},{17,25},{18,26},{19,27}} | collective-permute-start | bytes 1572872 | tf_op jit(solution)/shard_map/ppermute | solution.py:338
  7.1 14.0 %copy-start = (bf16[16,2048]{1,0:T(8,128)(2,1)S(1)}, bf16[16,2048]{1,0:T(8,128)(2,1)}, u32[]{:S(2)}) copy-start(bf16[16,2048]{1,0:T(8,128)(2,1)} %refs_0_) | copy-start | bytes 196612
  7.1 14.0 %copy-start.1 = (bf16[16,512]{1,0:T(8,128)(2,1)S(1)}, bf16[16,512]{1,0:T(8,128)(2,1)}, u32[]{:S(2)}) copy-start(bf16[16,512]{1,0:T(8,128)(2,1)} %refs_6_.1) | copy-start | bytes 49156
  7.2 14.0 %copy-start.2 = (bf16[16,512]{1,0:T(8,128)(2,1)S(1)}, bf16[16,512]{1,0:T(8,128)(2,1)}, u32[]{:S(2)}) copy-start(bf16[16,512]{1,0:T(8,128)(2,1)} %refs_7_.1) | copy-start | bytes 49156
  19.1 10.4 %collective-permute-start.4 = (bf16[2,1024,128]{2,1,0:T(8,128)(2,1)}, bf16[2,1024,128]{2,1,0:T(8,128)(2,1)S(1)}, u32[]{:S(2)}, u32[]{:S(2)}) collective-permute-start(bf16[2,1024,128]{2,1,0:T(8,128)(2,1)} %broadcast_select_fusion.1), channel_id=1, source_target_pairs={{8,4},{0,8},{9,5},{1,9},{10,6},{2,10},{11,7},{3,11},{24,20},{16,24... | collective-permute-start | bytes 1572872 | tf_op jit(solution)/shard_map/ppermute | solution.py:338
  19.8 16.1 %collective-permute-start.5 = (bf16[2,1024,128]{2,1,0:T(8,128)(2,1)S(1)}, bf16[2,1024,128]{2,1,0:T(8,128)(2,1)S(1)}, u32[]{:S(2)}, u32[]{:S(2)}) collective-permute-start(bf16[2,1024,128]{2,1,0:T(8,128)(2,1)S(1)} %collective-permute-done.3.refs_0_), channel_id=1, source_target_pairs={{8,12},{9,13},{10,14},{11,15},{24,28},{25,29},{26,30},{27,31}} | collective-permute-start | bytes 1572872 | tf_op jit(solution)/shard_map/ppermute | solution.py:338
  36.8 21.9 %collective-permute-start.6 = (bf16[2,1024,128]{2,1,0:T(8,128)(2,1)}, bf16[2,1024,128]{2,1,0:T(8,128)(2,1)S(1)}, u32[]{:S(2)}, u32[]{:S(2)}) collective-permute-start(bf16[2,1024,128]{2,1,0:T(8,128)(2,1)} %broadcast_select_fusion), channel_id=1, source_target_pairs={{0,4},{8,12},{1,5},{9,13},{2,6},{10,14},{3,7},{11,15},{16,20},{24,... | collective-permute-start | bytes 1572872 | tf_op jit(solution)/shard_map/ppermute | solution.py:338
  38.3 20.4 %collective-permute-start.7 = (f32[264,128]{1,0:T(8,128)S(1)}, f32[264,128]{1,0:T(8,128)S(1)}, u32[]{:S(2)}, u32[]{:S(2)}) collective-permute-start(f32[264,128]{1,0:T(8,128)S(1)} %get-tuple-element.62), channel_id=1, source_target_pairs={{0,4},{4,0},{8,12},{12,8},{1,5},{5,1},{9,13},{13,9},{2,6},{6,2},{1... | collective-permute-start | bytes 405512 | tf_op jit(solution)/shard_map/ppermute | solution.py:418
  41.0 17.7 %collective-permute-start.8 = (f32[264,128]{1,0:T(8,128)S(1)}, f32[264,128]{1,0:T(8,128)S(1)}, u32[]{:S(2)}, u32[]{:S(2)}) collective-permute-start(f32[264,128]{1,0:T(8,128)S(1)} %get-tuple-element.63), channel_id=1, source_target_pairs={{0,8},{4,12},{8,0},{12,4},{1,9},{5,13},{9,1},{13,5},{2,10},{6,14},... | collective-permute-start | bytes 405512 | tf_op jit(solution)/shard_map/ppermute | solution.py:418
  41.4 17.3 %collective-permute-start.9 = (f32[264,128]{1,0:T(8,128)S(1)}, f32[264,128]{1,0:T(8,128)S(1)}, u32[]{:S(2)}, u32[]{:S(2)}) collective-permute-start(f32[264,128]{1,0:T(8,128)S(1)} %get-tuple-element.64), channel_id=1, source_target_pairs={{0,12},{4,8},{8,4},{12,0},{1,13},{5,9},{9,5},{13,1},{2,14},{6,10},... | collective-permute-start | bytes 405512 | tf_op jit(solution)/shard_map/ppermute | solution.py:418

commit v2 on v1

--- a/solution.py
+++ b/solution.py
@@ -113,8 +113,8 @@
                 stat_ref[h, 1:2, columns] = jnp.sum(p, 0, keepdims=True)
 
 
-def anchor_kernel(pos_ref, q_ref, acc_ref, stat_ref, *refs, heads, copies, merge):
-    o_ref, *query_ref, k_ref, v_ref, vt_ref, sem = refs[-6:] if merge else refs[-5:]
+def anchor_kernel(pos_ref, q_ref, acc_ref, stat_ref, *refs, heads, copies):
+    o_ref, k_ref, v_ref, vt_ref, sem = refs[-5:]
     copy_refs = refs[:copies]
     first = pl.program_id(0) == 0
     rows = q_ref.shape[0]
@@ -130,13 +130,6 @@
                     act(pltpu.make_async_copy(ref.at[j], held, sem.at[j]))
 
     fetch(lambda copy: copy.start())
-    if merge:
-        returned = refs[copies : copies + merge["blocks"]]
-
-        @pl.when(first)
-        def _():
-            merge_parts(returned, query_ref[0], kv=merge["kv"], group=merge["group"])
-
     fetch(lambda copy: copy.wait())
 
     @pl.when(pos_ref[0] < 0)
@@ -263,6 +256,10 @@
         ).astype(BF16)
         for h in range(group):
             out_ref[:, (g * group + h) * HD : (g * group + h + 1) * HD] = out[h * share : (h + 1) * share]
+
+
+def merge_kernel(*refs, kv, group):
+    merge_parts(refs[:-1], refs[-1], kv=kv, group=group)
 
 
 def relay(blocks, last):
@@ -419,9 +416,8 @@
     ]
     returned = [partial[0]] + returned
 
-    context_out = query_out = None
+    context_out = None
     for g in range(kv):
-        last = g == kv - 1
         operands = [taken[g].reshape(1), *in_hbm(context_queries, *sums), *received[g]]
         in_specs = [
             pl.BlockSpec((rows, at_once * HD), lambda j, pos, g=g: (0, g * steps + j)),
@@ -430,11 +426,6 @@
         ] + [pl.BlockSpec(memory_space=pl.ANY)] * len(received[g])
         out_specs = [pl.BlockSpec((rows, at_once * HD), lambda j, pos, g=g: (0, g * steps + j))]
         out_shape = [jax.ShapeDtypeStruct((rows, heads * HD), BF16)]
-        if last:
-            operands += returned
-            in_specs += [pl.BlockSpec((payload_rows, HD), lambda j, pos: (0, 0))] * blocks
-            out_specs.append(pl.BlockSpec((share, heads * HD), lambda j, pos: (0, 0)))
-            out_shape.append(jax.ShapeDtypeStruct((share, heads * HD), BF16))
         if g > 0:
             operands += in_hbm(context_out)
             in_specs.append(pl.BlockSpec(memory_space=pl.ANY))
@@ -443,7 +434,6 @@
                 anchor_kernel,
                 heads=at_once,
                 copies=len(received[g]),
-                merge=dict(blocks=blocks, kv=kv, group=group) if last else None,
             ),
             grid_spec=pltpu.PrefetchScalarGridSpec(
                 num_scalar_prefetch=1,
@@ -466,7 +456,13 @@
             name="anchor",
         )(*operands)
         context_out = out[0]
-        query_out = out[-1]
+    context_out, returned = lax.optimization_barrier((context_out, returned))
+    query_out = pl.pallas_call(
+        functools.partial(merge_kernel, kv=kv, group=group),
+        out_shape=jax.ShapeDtypeStruct((share, heads * HD), BF16),
+        compiler_params=params,
+        name="merge",
+    )(*returned)
     return context_out, query_out
 
 

time: 70.3 us -> 67.9 us (0.966)
  the two profiles are of different devices: /device:TPU:26 before, /device:TPU:28 now
where the time goes in v2:
time: 67.9 us; the launch traced here: 67.4 us
  Pallas kernels  41.8 us (62%)
  starting transfers between devices  13.8 us (20%)
  waiting for transfers between devices  7.97 us (12%)
  other arithmetic  1.81 us (3%)
  local copies, waits for them, and re-layouts  1.3 us (2%)
  between operations  0.82 us (1%)
    pallas_call x2, Pallas kernels, body(): pl.pallas_call(functools.partial(anchor_kernel, heads=at_once, copies=len...  21.5 us
    pallas_call x2, Pallas kernels, own(): pl.pallas_call(functools.partial(own_kernel, heads=at_once), grid_spec=pl...  16.2 us
    ppermute x4, waiting for transfers between devices, step(): lax.ppermute(operand, 'ctx', [p for _, pairs in transfer for p in pairs])  7.96 us
    ppermute x3, starting transfers between devices, body(): lax.ppermute(partial[r], 'ctx', [(z, z ^ r) for z in range(blocks)])  5.18 us
    ppermute x3, starting transfers between devices, body(): lax.ppermute(query_queries, 'ctx', [(z, z ^ r) for z in range(blocks)])  4.45 us
    ppermute x4, starting transfers between devices, step(): lax.ppermute(operand, 'ctx', [p for _, pairs in transfer for p in pairs])  4.13 us
    pallas_call x1, Pallas kernels, body(): pl.pallas_call(functools.partial(partial_kernel, shares=blocks, kv=kv, gr...  3.25 us
  transfers between devices with their start and end apart: 10, of which 2 were waited for; matrix products, arithmetic and copies ran while one was open for 2% of the time, Pallas kernels for 61%

profile of v2, /device:TPU:28, one launch (start us, length us, event | category | flops | bytes accessed | tf_op | source)
XLA Modules:
  0.0 67.4 jit_solution(6355387209250391326)
XLA Ops:
  0.6 0.5 collective-permute-start
  1.1 0.3 collective-permute-start.1
  1.5 3.6 %collective-permute-start.2 = (bf16[16,2048]{1,0:T(8,128)(2,1)}, bf16[16,2048]{1,0:T(8,128)(2,1)S(1)}, u32[]{:S(2)}, u32[]{:S(2)}) collective-permute-start(bf16[16,2048]{1,0:T(8,128)(2,1)} %refs_0_), channel_id=1, source_target_pairs={{0,12},{4,8},{8,4},{12,0},{1,13},{5,9},{9,5},{13,1},{2,14},{6,10},... | collective-permute-start | bytes 196616 | tf_op jit(solution)/shard_map/ppermute | solution.py:377
  5.1 1.3 %dynamic-slice_bitcast_fusion = (bf16[1,1024,128]{2,1,0:T(8,128)(2,1)S(1)}, bf16[1,1024,128]{2,1,0:T(8,128)(2,1)S(1)}, bf16[1,1024,128]{2,1,0:T(8,128)(2,1)S(1)}, bf16[1,1024,128]{2,1,0:T(8,128)(2,1)S(1)}) fusion(bf16[1024,512]{1,0:T(8,128)(2,1)} %v_ref.3, s32[]{:T(128)S(6)} %select_n.46, s32[]{:T(128)S(6)} %select_n.44, bf16[1024,512]{1,0:T(8,128)(2,1)} %k_ref.3), kind=kLoop, calls=%fused_computation.4 | loop fusion | bytes 2097160 | tf_op jit(solution)/shard_map/stack | solution.py:297
  6.4 0.1 pad_maximum_fusion
  6.4 0.7 %collective-permute-start.3 = (bf16[2,1024,128]{2,1,0:T(8,128)(2,1)S(1)}, bf16[2,1024,128]{2,1,0:T(8,128)(2,1)S(1)}, u32[]{:S(2)}, u32[]{:S(2)}) collective-permute-start(bf16[2,1024,128]{2,1,0:T(8,128)(2,1)S(1)} %pad_maximum_fusion), channel_id=1, source_target_pairs={{0,8},{1,9},{2,10},{3,11},{16,24},{17,25},{18,26},{19,27}} | collective-permute-start | bytes 1572872 | tf_op jit(solution)/shard_map/ppermute | solution.py:335
  7.1 0.0 copy-start
  7.1 0.0 copy-start.1
  7.2 0.0 copy-start.2
  7.2 11.0 %own.2 = (f32[16,128,1024]{2,1,0:T(8,128)}, f32[16,2,1024]{2,1,0:T(2,128)}) custom-call(s32[1]{0:T(128)} %bitcast.1.off_ref, bf16[1024,2048]{1,0:T(8,128)(2,1)} %q_ref.6, bf16[1024,512]{1,0:T(8,128)(2,1)} %k_ref.3, bf16[1024,512]{1,0:T(8,128)(2,1)} %v_ref.3), custom_call_target="tpu_custom_call" | custom-call | flops 6442450944 | bytes 12582912 | tf_op jit(solution)/shard_map/own/pallas_call | solution.py:348
  18.2 0.0 collective-permute-done.refs_1_
  18.2 0.0 collective-permute-done.1.refs_2_
  18.2 0.0 collective-permute-done.2.refs_3_
  18.2 0.0 collective-permute-done.3.refs_0_
  18.2 0.9 %broadcast_select_fusion.1 = bf16[2,1024,128]{2,1,0:T(8,128)(2,1)} fusion(bf16[2,1024,128]{2,1,0:T(8,128)(2,1)S(1)} %collective-permute-done.3.refs_0_, pred[]{:T(512)S(6)} %eq.19, bf16[1,1024,128]{2,1,0:T(8,128)(2,1)S(1)} %get-tuple-element.80, bf16[1,1024,128]{2,1,0:T(8,128)(2,1)S(1)} %get-tuple-element.83), kind=kLoop, calls=%fused_computation.3 | loop fusion | flops 524288 | bytes 1572865 | tf_op jit(solution)/shard_map/jit(_where)/select_n | solution.py:334
  19.1 0.7 %collective-permute-start.4 = (bf16[2,1024,128]{2,1,0:T(8,128)(2,1)}, bf16[2,1024,128]{2,1,0:T(8,128)(2,1)S(1)}, u32[]{:S(2)}, u32[]{:S(2)}) collective-permute-start(bf16[2,1024,128]{2,1,0:T(8,128)(2,1)} %broadcast_select_fusion.1), channel_id=1, source_target_pairs={{8,4},{0,8},{9,5},{1,9},{10,6},{2,10},{11,7},{3,11},{24,20},{16,24... | collective-permute-start | bytes 1572872 | tf_op jit(solution)/shard_map/ppermute | solution.py:335
  19.8 1.3 %collective-permute-start.5 = (bf16[2,1024,128]{2,1,0:T(8,128)(2,1)S(1)}, bf16[2,1024,128]{2,1,0:T(8,128)(2,1)S(1)}, u32[]{:S(2)}, u32[]{:S(2)}) collective-permute-start(bf16[2,1024,128]{2,1,0:T(8,128)(2,1)S(1)} %collective-permute-done.3.refs_0_), channel_id=1, source_target_pairs={{8,12},{9,13},{10,14},{11,15},{24,28},{25,29},{26,30},{27,31}} | collective-permute-start | bytes 1572872 | tf_op jit(solution)/shard_map/ppermute | solution.py:335
  21.1 3.2 %partial.1 = (f32[264,128]{1,0:T(8,128)S(1)}, f32[264,128]{1,0:T(8,128)S(1)}, f32[264,128]{1,0:T(8,128)S(1)}, f32[264,128]{1,0:T(8,128)S(1)}) custom-call(s32[1]{0:T(128)} %bitcast.2.lanes_ref, s32[1]{0:T(128)} %bitcast.3.mine_ref, bf16[16,2048]{1,0:T(8,128)(2,1)S(1)} %copy-done, bf16[16,2048]{1,0:T(8,128)(2,1)S(1)} %collective-permute-done.refs_1_, ...), custom_call_target="tpu_custom_call" | custom-call | tf_op jit(solution)/shard_map/partial/pallas_call | solution.py:387
  24.4 5.1 %own.3 = (f32[16,128,1024]{2,1,0:T(8,128)}, f32[16,2,1024]{2,1,0:T(2,128)}) custom-call(s32[1]{0:T(128)} %bitcast.1.off_ref, bf16[1024,2048]{1,0:T(8,128)(2,1)} %q_ref.6, bf16[1024,512]{1,0:T(8,128)(2,1)} %k_ref.3, bf16[1024,512]{1,0:T(8,128)(2,1)} %v_ref.3, ...), custom_call_target="tpu_custom_call", output_to_operand_aliasing={{0}: (4, {}), {1}: (5, {})} | custom-call | flops 2147483648 | bytes 4194304 | tf_op jit(solution)/shard_map/own/pallas_call | solution.py:348
  29.5 0.0 collective-permute-done.4.refs_1_.refs_0_
  29.5 6.4 %collective-permute-done.5.refs_2_ = bf16[2,1024,128]{2,1,0:T(8,128)(2,1)S(1)} collective-permute-done((bf16[2,1024,128]{2,1,0:T(8,128)(2,1)S(1)}, bf16[2,1024,128]{2,1,0:T(8,128)(2,1)S(1)}, u32[]{:S(2)}, u32[]{:S(2)}) %collective-permute-start.5) | collective-permute-done | bytes 524320 | tf_op jit(solution)/shard_map/ppermute | solution.py:335
  35.9 0.9 %broadcast_select_fusion = bf16[2,1024,128]{2,1,0:T(8,128)(2,1)} fusion(bf16[2,1024,128]{2,1,0:T(8,128)(2,1)S(1)} %collective-permute-done.4.refs_1_.refs_0_, pred[]{:T(512)S(6)} %eq.19, bf16[1,1024,128]{2,1,0:T(8,128)(2,1)S(1)} %get-tuple-element.80, bf16[1,1024,128]{2,1,0:T(8,128)(2,1)S(1)} %get-tuple-element.83), kind=kLoop, calls=%fused_computation.2 | loop fusion | flops 524288 | bytes 1572865 | tf_op jit(solution)/shard_map/jit(_where)/select_n | solution.py:345
  36.8 1.5 %collective-permute-start.6 = (bf16[2,1024,128]{2,1,0:T(8,128)(2,1)}, bf16[2,1024,128]{2,1,0:T(8,128)(2,1)S(1)}, u32[]{:S(2)}, u32[]{:S(2)}) collective-permute-start(bf16[2,1024,128]{2,1,0:T(8,128)(2,1)} %broadcast_select_fusion), channel_id=1, source_target_pairs={{0,4},{8,12},{1,5},{9,13},{2,6},{10,14},{3,7},{11,15},{16,20},{24,... | collective-permute-start | bytes 1572872 | tf_op jit(solution)/shard_map/ppermute | solution.py:335
  38.3 2.7 %collective-permute-start.7 = (f32[264,128]{1,0:T(8,128)S(1)}, f32[264,128]{1,0:T(8,128)S(1)}, u32[]{:S(2)}, u32[]{:S(2)}) collective-permute-start(f32[264,128]{1,0:T(8,128)S(1)} %get-tuple-element.70), channel_id=1, source_target_pairs={{0,4},{4,0},{8,12},{12,8},{1,5},{5,1},{9,13},{13,9},{2,6},{6,2},{1... | collective-permute-start | bytes 405512 | tf_op jit(solution)/shard_map/ppermute | solution.py:415
  41.0 0.4 collective-permute-start.8
  41.4 2.1 %collective-permute-start.9 = (f32[264,128]{1,0:T(8,128)S(1)}, f32[264,128]{1,0:T(8,128)S(1)}, u32[]{:S(2)}, u32[]{:S(2)}) collective-permute-start(f32[264,128]{1,0:T(8,128)S(1)} %get-tuple-element.72), channel_id=1, source_target_pairs={{0,12},{4,8},{8,4},{12,0},{1,13},{5,9},{9,5},{13,1},{2,14},{6,10},... | collective-permute-start | bytes 405512 | tf_op jit(solution)/shard_map/ppermute | solution.py:415
  43.5 10.8 %anchor.2.refs_2_ = bf16[1024,2048]{1,0:T(8,128)(2,1)} custom-call(s32[1]{0:T(128)} %bitcast.8.pos_ref, bf16[1024,2048]{1,0:T(8,128)(2,1)} %q_ref.6, f32[16,128,1024]{2,1,0:T(8,128)} %get-tuple-element.63.acc_ref, f32[16,2,1024]{2,1,0:T(2,128)} %get-tuple-element.64.stat_ref, bf16[2,1024,128]{2,1,0:T(8,128)(2,1)S(1)} %collective-permute-done.3.refs_0_, ...), custom_call_target="tpu_custom_call" | custom-call | flops 4294967296 | bytes 8388608 | tf_op jit(solution)/shard_map/anchor/pallas_call | solution.py:432
  54.2 1.6 %collective-permute-done.6.refs_1_ = bf16[2,1024,128]{2,1,0:T(8,128)(2,1)S(1)} collective-permute-done((bf16[2,1024,128]{2,1,0:T(8,128)(2,1)}, bf16[2,1024,128]{2,1,0:T(8,128)(2,1)S(1)}, u32[]{:S(2)}, u32[]{:S(2)}) %collective-permute-start.6) | collective-permute-done | bytes 524320 | tf_op jit(solution)/shard_map/ppermute | solution.py:335
  55.8 10.7 %anchor.3 = bf16[1024,2048]{1,0:T(8,128)(2,1)} custom-call(s32[1]{0:T(128)} %bitcast.pos_ref, bf16[1024,2048]{1,0:T(8,128)(2,1)} %q_ref.6, f32[16,128,1024]{2,1,0:T(8,128)} %get-tuple-element.63.acc_ref, f32[16,2,1024]{2,1,0:T(2,128)} %get-tuple-element.64.stat_ref, ...), custom_call_target="tpu_custom_call", output_to_operand_aliasing={{}: (6, {})} | custom-call | flops 4294967296 | bytes 8388608 | tf_op jit(solution)/shard_map/anchor/pallas_call | solution.py:432
  66.5 0.0 collective-permute-done.7.refs_1_
  66.5 0.0 collective-permute-done.8.refs_2_
  66.6 0.9 %merge.1 = bf16[16,2048]{1,0:T(8,128)(2,1)} custom-call(f32[264,128]{1,0:T(8,128)S(1)} %get-tuple-element.74.refs_0_, f32[264,128]{1,0:T(8,128)S(1)} %collective-permute-done.7.refs_1_, f32[264,128]{1,0:T(8,128)S(1)} %collective-permute-done.8.refs_2_, f32[264,128]{1,0:T(8,128)S(1)} %collective-permute-done.9.refs_3_), custom_call_target="tpu_custom_call" | custom-call | tf_op jit(solution)/shard_map/merge/pallas_call | solution.py:460
  (4 shorter events, 0.0 us)
Async XLA Ops:
  0.6 17.6 %collective-permute-start = (bf16[16,2048]{1,0:T(8,128)(2,1)}, bf16[16,2048]{1,0:T(8,128)(2,1)S(1)}, u32[]{:S(2)}, u32[]{:S(2)}) collective-permute-start(bf16[16,2048]{1,0:T(8,128)(2,1)} %refs_0_), channel_id=1, source_target_pairs={{0,4},{4,0},{8,12},{12,8},{1,5},{5,1},{9,13},{13,9},{2,6},{6,2},{1... | collective-permute-start | bytes 196616 | tf_op jit(solution)/shard_map/ppermute | solution.py:377
  1.1 17.1 %collective-permute-start.1 = (bf16[16,2048]{1,0:T(8,128)(2,1)}, bf16[16,2048]{1,0:T(8,128)(2,1)S(1)}, u32[]{:S(2)}, u32[]{:S(2)}) collective-permute-start(bf16[16,2048]{1,0:T(8,128)(2,1)} %refs_0_), channel_id=1, source_target_pairs={{0,8},{4,12},{8,0},{12,4},{1,9},{5,13},{9,1},{13,5},{2,10},{6,14},... | collective-permute-start | bytes 196616 | tf_op jit(solution)/shard_map/ppermute | solution.py:377
  1.5 16.7 %collective-permute-start.2 = (bf16[16,2048]{1,0:T(8,128)(2,1)}, bf16[16,2048]{1,0:T(8,128)(2,1)S(1)}, u32[]{:S(2)}, u32[]{:S(2)}) collective-permute-start(bf16[16,2048]{1,0:T(8,128)(2,1)} %refs_0_), channel_id=1, source_target_pairs={{0,12},{4,8},{8,4},{12,0},{1,13},{5,9},{9,5},{13,1},{2,14},{6,10},... | collective-permute-start | bytes 196616 | tf_op jit(solution)/shard_map/ppermute | solution.py:377
  6.4 11.8 %collective-permute-start.3 = (bf16[2,1024,128]{2,1,0:T(8,128)(2,1)S(1)}, bf16[2,1024,128]{2,1,0:T(8,128)(2,1)S(1)}, u32[]{:S(2)}, u32[]{:S(2)}) collective-permute-start(bf16[2,1024,128]{2,1,0:T(8,128)(2,1)S(1)} %pad_maximum_fusion), channel_id=1, source_target_pairs={{0,8},{1,9},{2,10},{3,11},{16,24},{17,25},{18,26},{19,27}} | collective-permute-start | bytes 1572872 | tf_op jit(solution)/shard_map/ppermute | solution.py:335
  7.1 14.0 %copy-start = (bf16[16,2048]{1,0:T(8,128)(2,1)S(1)}, bf16[16,2048]{1,0:T(8,128)(2,1)}, u32[]{:S(2)}) copy-start(bf16[16,2048]{1,0:T(8,128)(2,1)} %refs_0_) | copy-start | bytes 196612
  7.1 14.0 %copy-start.1 = (bf16[16,512]{1,0:T(8,128)(2,1)S(1)}, bf16[16,512]{1,0:T(8,128)(2,1)}, u32[]{:S(2)}) copy-start(bf16[16,512]{1,0:T(8,128)(2,1)} %refs_6_.1) | copy-start | bytes 49156
  7.2 14.0 %copy-start.2 = (bf16[16,512]{1,0:T(8,128)(2,1)S(1)}, bf16[16,512]{1,0:T(8,128)(2,1)}, u32[]{:S(2)}) copy-start(bf16[16,512]{1,0:T(8,128)(2,1)} %refs_7_.1) | copy-start | bytes 49156
  19.1 10.4 %collective-permute-start.4 = (bf16[2,1024,128]{2,1,0:T(8,128)(2,1)}, bf16[2,1024,128]{2,1,0:T(8,128)(2,1)S(1)}, u32[]{:S(2)}, u32[]{:S(2)}) collective-permute-start(bf16[2,1024,128]{2,1,0:T(8,128)(2,1)} %broadcast_select_fusion.1), channel_id=1, source_target_pairs={{8,4},{0,8},{9,5},{1,9},{10,6},{2,10},{11,7},{3,11},{24,20},{16,24... | collective-permute-start | bytes 1572872 | tf_op jit(solution)/shard_map/ppermute | solution.py:335
  19.8 16.1 %collective-permute-start.5 = (bf16[2,1024,128]{2,1,0:T(8,128)(2,1)S(1)}, bf16[2,1024,128]{2,1,0:T(8,128)(2,1)S(1)}, u32[]{:S(2)}, u32[]{:S(2)}) collective-permute-start(bf16[2,1024,128]{2,1,0:T(8,128)(2,1)S(1)} %collective-permute-done.3.refs_0_), channel_id=1, source_target_pairs={{8,12},{9,13},{10,14},{11,15},{24,28},{25,29},{26,30},{27,31}} | collective-permute-start | bytes 1572872 | tf_op jit(solution)/shard_map/ppermute | solution.py:335
  36.8 19.0 %collective-permute-start.6 = (bf16[2,1024,128]{2,1,0:T(8,128)(2,1)}, bf16[2,1024,128]{2,1,0:T(8,128)(2,1)S(1)}, u32[]{:S(2)}, u32[]{:S(2)}) collective-permute-start(bf16[2,1024,128]{2,1,0:T(8,128)(2,1)} %broadcast_select_fusion), channel_id=1, source_target_pairs={{0,4},{8,12},{1,5},{9,13},{2,6},{10,14},{3,7},{11,15},{16,20},{24,... | collective-permute-start | bytes 1572872 | tf_op jit(solution)/shard_map/ppermute | solution.py:335
  38.3 28.2 %collective-permute-start.7 = (f32[264,128]{1,0:T(8,128)S(1)}, f32[264,128]{1,0:T(8,128)S(1)}, u32[]{:S(2)}, u32[]{:S(2)}) collective-permute-start(f32[264,128]{1,0:T(8,128)S(1)} %get-tuple-element.70), channel_id=1, source_target_pairs={{0,4},{4,0},{8,12},{12,8},{1,5},{5,1},{9,13},{13,9},{2,6},{6,2},{1... | collective-permute-start | bytes 405512 | tf_op jit(solution)/shard_map/ppermute | solution.py:415
  41.0 25.5 %collective-permute-start.8 = (f32[264,128]{1,0:T(8,128)S(1)}, f32[264,128]{1,0:T(8,128)S(1)}, u32[]{:S(2)}, u32[]{:S(2)}) collective-permute-start(f32[264,128]{1,0:T(8,128)S(1)} %get-tuple-element.71), channel_id=1, source_target_pairs={{0,8},{4,12},{8,0},{12,4},{1,9},{5,13},{9,1},{13,5},{2,10},{6,14},... | collective-permute-start | bytes 405512 | tf_op jit(solution)/shard_map/ppermute | solution.py:415
  41.4 25.2 %collective-permute-start.9 = (f32[264,128]{1,0:T(8,128)S(1)}, f32[264,128]{1,0:T(8,128)S(1)}, u32[]{:S(2)}, u32[]{:S(2)}) collective-permute-start(f32[264,128]{1,0:T(8,128)S(1)} %get-tuple-element.72), channel_id=1, source_target_pairs={{0,12},{4,8},{8,4},{12,0},{1,13},{5,9},{9,5},{13,1},{2,14},{6,10},... | collective-permute-start | bytes 405512 | tf_op jit(solution)/shard_map/ppermute | solution.py:415
